TPU v7x, 128 devices: a whole 4x4x4 slice. The times are simulated.
128 devices in a mesh: row: 8 (over x, core), col: 16 (over y, z).
Axes of the slice: x: 4, y: 4, z: 4, core: 2. Of those that a mesh axis runs over, the one named last changes fastest.
Arguments:
- child_update: bfloat16 [8, 8, 256, 2, 4096], P('row', None, None, None, 'col'), may hold values from -0.41992188 to 0.41992188
- front: float32 [12288, 12288], P('row', 'col')
- pivot_inverses: bfloat16 [8, 256, 256], replicated
- child_maps: int32 [2, 32], replicated, may hold values from 0 to 47, as said below
Outputs:
- front_out: float32 [12288, 12288], P('row', 'col')
- factor: bfloat16 [12288, 2048], P('row', 'col')
Inputs may be any that keep to these rules, and one draw needn't show every extreme that they name: Each row of child_maps is strictly increasing, and holds every one of the 6 parent tiles g * 6 .. (g + 1) * 6 - 1 for some g.
All inputs are finite; a program needn't handle non-finite values.
Results may differ from a plain program's by a relative error of at most 0.033.
Values may be sent and summed in bfloat16 or wider, within the bound.
A program may use at most 192 MiB of HBM per device.

v0:
```python
import jax
import jax.numpy as jnp
from jax import lax
from jax.sharding import PartitionSpec as P


def broadcast(block, axis, holder):
    block = jnp.where(lax.axis_index(axis) == holder, block, jnp.zeros_like(block))
    return lax.psum(block, axis)


def slot_plan(mapping, residue, row_step, row_tiles, own_rows):
    positions = jnp.arange(row_tiles, dtype=jnp.int32)
    targets = mapping[residue + row_step * positions]
    owners = targets // own_rows
    earlier = (owners[:, None] == owners[None, :]) & (positions[None, :] < positions[:, None])
    before = jnp.sum(earlier.astype(jnp.int32), axis=1)
    return (targets, owners, before)


def row_sender(block, my_map, row_pos, row_step, row_tiles, own_rows, rows_grid, slot_count):
    targets, owners, before = slot_plan(my_map, row_pos % row_step, row_step, row_tiles, own_rows)
    pick = (owners[None, None, :] == jnp.arange(rows_grid)[:, None, None]) & (
        before[None, None, :] == jnp.arange(slot_count)[None, :, None]
    )
    return jnp.einsum(
        "dqi,ipm->dqpm", pick.astype(jnp.bfloat16), block, preferred_element_type=jnp.float32
    ).astype(jnp.bfloat16)


def row_selector(child_maps, row_pos, row_step, row_tiles, own_rows, rows_grid, slot_count):

    def per_source(source):
        return slot_plan(
            child_maps[source // row_step], source % row_step, row_step, row_tiles, own_rows
        )

    targets, owners, before = jax.vmap(per_source)(jnp.arange(rows_grid, dtype=jnp.int32))
    wanted = row_pos * own_rows + jnp.arange(own_rows, dtype=jnp.int32)
    match = (targets[None, :, None, :] == wanted[:, None, None, None]) & (
        before[None, :, None, :] == jnp.arange(slot_count)[None, None, :, None]
    )
    return jnp.sum(match.astype(jnp.int32), axis=3).astype(jnp.bfloat16)


def column_sender(mapping, col_pos, cols_grid, col_span, own_cols):
    mine = mapping[col_pos + cols_grid * jnp.arange(col_span, dtype=jnp.int32)]
    return (mine[None, :] // own_cols == jnp.arange(cols_grid)[:, None]).astype(jnp.bfloat16)


def column_selector(mapping, col_pos, cols_grid, col_span, own_cols):
    source_tiles = (
        jnp.arange(cols_grid, dtype=jnp.int32)[:, None]
        + cols_grid * jnp.arange(col_span, dtype=jnp.int32)[None, :]
    )
    targets = mapping[source_tiles]
    wanted = col_pos * own_cols + jnp.arange(own_cols, dtype=jnp.int32)
    return jnp.sum((targets[None, :, :] == wanted[:, None, None]).astype(jnp.int32), axis=2).astype(
        jnp.bfloat16
    )


def per_device(child_update, front, pivot_inverses, child_maps):
    rows_grid = lax.axis_size("row")
    cols_grid = lax.axis_size("col")
    row_pos = lax.axis_index("row")
    col_pos = lax.axis_index("col")
    tile_size = pivot_inverses.shape[1]
    row_step = rows_grid // 2
    row_tiles = child_update.shape[1]
    col_span = child_update.shape[3]
    rows_dev, cols_dev = front.shape
    own_rows = rows_dev // tile_size
    own_cols = cols_dev // tile_size
    slot_count = (own_rows + row_step - 1) // row_step
    my_tiles = child_update[0]
    my_child = row_pos // row_step
    my_map = child_maps[my_child]
    row_select = row_selector(
        child_maps, row_pos, row_step, row_tiles, own_rows, rows_grid, slot_count
    )
    strips = my_tiles.reshape(row_tiles, tile_size, col_span * tile_size)
    row_send = row_sender(
        strips, my_map, row_pos, row_step, row_tiles, own_rows, rows_grid, slot_count
    )
    row_recv = lax.all_to_all(row_send, "row", split_axis=0, concat_axis=0, tiled=True)
    child_mask = (jnp.arange(rows_grid)[None, :] // row_step == jnp.arange(2)[:, None]).astype(
        jnp.bfloat16
    )
    per_child = jnp.einsum(
        "lsq,ks,sqpm->klpm", row_select, child_mask, row_recv, preferred_element_type=jnp.float32
    ).astype(jnp.bfloat16)
    per_child = per_child.reshape(2, rows_dev, col_span, tile_size)
    outgoing = jnp.stack(
        [
            column_sender(child_maps[0], col_pos, cols_grid, col_span, own_cols),
            column_sender(child_maps[1], col_pos, cols_grid, col_span, own_cols),
        ],
        axis=0,
    )
    col_send = jnp.einsum(
        "kdh,kphq->dkpq", outgoing, per_child, preferred_element_type=jnp.float32
    ).astype(jnp.bfloat16)
    col_recv = lax.all_to_all(col_send, "col", split_axis=0, concat_axis=0, tiled=True)
    col_select = jnp.stack(
        [
            column_selector(child_maps[0], col_pos, cols_grid, col_span, own_cols),
            column_selector(child_maps[1], col_pos, cols_grid, col_span, own_cols),
        ],
        axis=2,
    )
    added = jnp.einsum("jsk,skpq->pjq", col_select, col_recv, preferred_element_type=jnp.float32)
    assembled = front + added.reshape(rows_dev, cols_dev)
    current = assembled
    blocks = []
    for block_idx in range(pivot_inverses.shape[0]):
        start_col = block_idx * tile_size
        col_root = start_col // cols_dev
        col_offset = start_col % cols_dev
        row_root = start_col // rows_dev
        row_offset = start_col % rows_dev
        row_panel = broadcast(
            current[row_offset : row_offset + tile_size, :].astype(jnp.bfloat16), "row", row_root
        )
        column_panel = broadcast(
            current[:, col_offset : col_offset + tile_size].astype(jnp.bfloat16), "col", col_root
        )
        factor_block = jnp.dot(
            column_panel, pivot_inverses[block_idx], preferred_element_type=jnp.float32
        ).astype(jnp.bfloat16)
        current = current - jnp.dot(factor_block, row_panel, preferred_element_type=jnp.float32)
        blocks.append(factor_block)
    factor_all = jnp.concatenate(blocks, axis=1)
    factor_width = factor_all.shape[1] // cols_grid
    factor = lax.dynamic_slice_in_dim(factor_all, col_pos * factor_width, factor_width, 1)
    return (current, factor)


def solution(mesh):
    placed = (P("row", None, None, None, "col"), P("row", "col"), P(), P())
    return jax.shard_map(
        per_device,
        mesh=mesh,
        in_specs=placed,
        out_specs=(P("row", "col"), P("row", "col")),
        check_vma=False,
    )
```

profile of v0, /device:TPU:0, one launch (start us, length us, event | category | flops | bytes accessed | tf_op | source)
XLA Modules:
  0.0 1921.8 jit_solution(1208781261729666682)
XLA Ops:
  8.9 3.2 reshape_squeeze.3
  13.5 3.5 copy.33
  17.0 4.7 all-to-all-start
  25.6 45.8 %all-to-all-done = bf16[8,2,256,512]{3,2,1,0:T(8,128)(2,1)} async-done(((bf16[8,2,256,512]{3,2,1,0:T(8,128)(2,1)}), bf16[8,2,256,512]{3,2,1,0:T(8,128)(2,1)}, u32[]{:S(2)}, u32[]{:S(2)}) %all-to-all-start) | async-done | bytes 4194336 | tf_op jit(solution)/shard_map/all_to_all | solution.py:86
  71.3 21.8 %fusion.4 = bf16[8,256,512,6]{2,3,1,0:T(8,128)(2,1)} fusion(bf16[6,8,2,1]{0,2,3,1:T(2,128)(2,1)S(1)} %copy.47, bf16[8,2,256,512]{3,2,1,0:T(8,128)(2,1)} %all-to-all-done), kind=kOutput, calls=%fused_computation.12 | convolution fusion | flops 25165824 | bytes 16777408 | tf_op jit(solution)/shard_map/lsq,ks,sqpm->klpm/dot_general | solution.py:90
  93.1 13.5 fusion.9
  106.7 3.8 copy.52
  110.5 8.5 reshape.553
  118.9 11.3 convert_bitcast_fusion
  130.3 35.9 %copy.39 = bf16[16,2,1536,256]{3,1,2,0:T(2,128)(2,1)} copy(bf16[16,2,1536,256]{3,0,1,2:T(8,128)(2,1)} %convert_bitcast_fusion) | data formatting | bytes 50331648 | tf_op jit(solution)/shard_map/convert_element_type | solution.py:103
  166.1 8.2 all-to-all-start.1
  176.4 454.1 %all-to-all-done.1 = bf16[16,2,1536,256]{3,1,2,0:T(2,128)(2,1)} async-done(((bf16[16,2,1536,256]{3,1,2,0:T(2,128)(2,1)}), bf16[16,2,1536,256]{3,1,2,0:T(2,128)(2,1)}, u32[]{:S(2)}, u32[]{:S(2)}) %all-to-all-start.1) | async-done | bytes 25165856 | tf_op jit(solution)/shard_map/all_to_all | solution.py:104
  630.4 26.1 %fusion.12 = f32[1536,3,256]{2,1,0:T(4,128)} fusion(bf16[16,2,1536,256]{3,1,2,0:T(2,128)(2,1)} %all-to-all-done.1, bf16[3,16,1]{1,0,2:T(4,128)(2,1)S(1)} %get-tuple-element.53, bf16[3,16,1]{1,0,2:T(4,128)(2,1)S(1)} %get-tuple-element.54), kind=kOutput, calls=%fused_computation.24 | convolution fusion | flops 75497856 | bytes 29884608 | tf_op jit(solution)/shard_map/jsk,skpq->pjq/dot_general | solution.py:112
  656.5 6.9 copy.43
  663.4 6.0 copy.44
  669.4 6.6 fusion.58
  678.2 88.8 %all-reduce.18.cloned.1.call-done = bf16[1536,256]{1,0:T(8,128)(2,1)} async-done(((bf16[1536,256]{1,0:T(8,128)(2,1)}), bf16[1536,256]{1,0:T(8,128)(2,1)}) %all-reduce.18.cloned.1.call-update) | async-done | bytes 786448 | tf_op jit(solution)/shard_map/psum | solution.py:9
  767.0 2.4 constant_dynamic-update-slice_fusion.7
  769.4 60.0 %all-reduce.20.cloned.1.call-done = bf16[256,768]{1,0:T(8,128)(2,1)} async-done(((bf16[256,768]{1,0:T(8,128)(2,1)}), bf16[256,768]{1,0:T(8,128)(2,1)}) %all-reduce.20.cloned.1.call-update) | async-done | bytes 393232 | tf_op jit(solution)/shard_map/psum | solution.py:9
  829.5 5.5 fusion.59
  836.8 84.7 %all-reduce.22.cloned.1.call-done = bf16[1536,256]{1,0:T(8,128)(2,1)} async-done(((bf16[1536,256]{1,0:T(8,128)(2,1)}), bf16[1536,256]{1,0:T(8,128)(2,1)}) %all-reduce.22.cloned.1.call-update) | async-done | bytes 786448 | tf_op jit(solution)/shard_map/psum | solution.py:9
  921.5 2.5 constant_dynamic-update-slice_fusion.6
  924.0 59.9 %all-reduce.24.cloned.1.call-done = bf16[256,768]{1,0:T(8,128)(2,1)} async-done(((bf16[256,768]{1,0:T(8,128)(2,1)}), bf16[256,768]{1,0:T(8,128)(2,1)}) %all-reduce.24.cloned.1.call-update) | async-done | bytes 393232 | tf_op jit(solution)/shard_map/psum | solution.py:9
  983.8 5.5 fusion.60
  991.2 84.6 %all-reduce.26.cloned.1.call-done = bf16[1536,256]{1,0:T(8,128)(2,1)} async-done(((bf16[1536,256]{1,0:T(8,128)(2,1)}), bf16[1536,256]{1,0:T(8,128)(2,1)}) %all-reduce.26.cloned.1.call-update) | async-done | bytes 786448 | tf_op jit(solution)/shard_map/psum | solution.py:9
  1075.8 2.4 constant_dynamic-update-slice_fusion.5
  1078.3 59.9 %all-reduce.28.cloned.1.call-done = bf16[256,768]{1,0:T(8,128)(2,1)} async-done(((bf16[256,768]{1,0:T(8,128)(2,1)}), bf16[256,768]{1,0:T(8,128)(2,1)}) %all-reduce.28.cloned.1.call-update) | async-done | bytes 393232 | tf_op jit(solution)/shard_map/psum | solution.py:9
  1138.2 5.5 fusion.61
  1145.5 84.6 %all-reduce.30.cloned.1.call-done = bf16[1536,256]{1,0:T(8,128)(2,1)} async-done(((bf16[1536,256]{1,0:T(8,128)(2,1)}), bf16[1536,256]{1,0:T(8,128)(2,1)}) %all-reduce.30.cloned.1.call-update) | async-done | bytes 786448 | tf_op jit(solution)/shard_map/psum | solution.py:9
  1230.2 2.4 constant_dynamic-update-slice_fusion.4
  1232.6 60.1 %all-reduce.32.cloned.1.call-done = bf16[256,768]{1,0:T(8,128)(2,1)} async-done(((bf16[256,768]{1,0:T(8,128)(2,1)}), bf16[256,768]{1,0:T(8,128)(2,1)}) %all-reduce.32.cloned.1.call-update) | async-done | bytes 393232 | tf_op jit(solution)/shard_map/psum | solution.py:9
  1292.7 5.5 fusion.62
  1300.0 84.6 %all-reduce.34.cloned.1.call-done = bf16[1536,256]{1,0:T(8,128)(2,1)} async-done(((bf16[1536,256]{1,0:T(8,128)(2,1)}), bf16[1536,256]{1,0:T(8,128)(2,1)}) %all-reduce.34.cloned.1.call-update) | async-done | bytes 786448 | tf_op jit(solution)/shard_map/psum | solution.py:9
  1384.6 2.5 constant_dynamic-update-slice_fusion.3
  1387.1 59.8 %all-reduce.36.cloned.1.call-done = bf16[256,768]{1,0:T(8,128)(2,1)} async-done(((bf16[256,768]{1,0:T(8,128)(2,1)}), bf16[256,768]{1,0:T(8,128)(2,1)}) %all-reduce.36.cloned.1.call-update) | async-done | bytes 393232 | tf_op jit(solution)/shard_map/psum | solution.py:9
  1446.9 5.5 fusion.63
  1454.3 84.6 %all-reduce.38.cloned.1.call-done = bf16[1536,256]{1,0:T(8,128)(2,1)} async-done(((bf16[1536,256]{1,0:T(8,128)(2,1)}), bf16[1536,256]{1,0:T(8,128)(2,1)}) %all-reduce.38.cloned.1.call-update) | async-done | bytes 786448 | tf_op jit(solution)/shard_map/psum | solution.py:9
  1538.9 2.4 constant_dynamic-update-slice_fusion.2
  1541.4 59.9 %all-reduce.40.cloned.1.call-done = bf16[256,768]{1,0:T(8,128)(2,1)} async-done(((bf16[256,768]{1,0:T(8,128)(2,1)}), bf16[256,768]{1,0:T(8,128)(2,1)}) %all-reduce.40.cloned.1.call-update) | async-done | bytes 393232 | tf_op jit(solution)/shard_map/psum | solution.py:9
  1601.3 5.5 fusion.64
  1608.6 84.7 %all-reduce.42.cloned.1.call-done = bf16[1536,256]{1,0:T(8,128)(2,1)} async-done(((bf16[1536,256]{1,0:T(8,128)(2,1)}), bf16[1536,256]{1,0:T(8,128)(2,1)}) %all-reduce.42.cloned.1.call-update) | async-done | bytes 786448 | tf_op jit(solution)/shard_map/psum | solution.py:9
  1693.3 2.5 constant_dynamic-update-slice_fusion.1
  1695.7 59.9 %all-reduce.44.cloned.1.call-done = bf16[256,768]{1,0:T(8,128)(2,1)} async-done(((bf16[256,768]{1,0:T(8,128)(2,1)}), bf16[256,768]{1,0:T(8,128)(2,1)}) %all-reduce.44.cloned.1.call-update) | async-done | bytes 393232 | tf_op jit(solution)/shard_map/psum | solution.py:9
  1755.6 5.5 fusion.65
  1763.0 84.7 %all-reduce.46.cloned.1.call-done = bf16[1536,256]{1,0:T(8,128)(2,1)} async-done(((bf16[1536,256]{1,0:T(8,128)(2,1)}), bf16[1536,256]{1,0:T(8,128)(2,1)}) %all-reduce.46.cloned.1.call-update) | async-done | bytes 786448 | tf_op jit(solution)/shard_map/psum | solution.py:9
  1847.6 2.4 constant_dynamic-update-slice_fusion
  1852.0 57.3 %all-reduce.48.cloned.1.call-done = bf16[256,768]{1,0:T(8,128)(2,1)} async-done(((bf16[256,768]{1,0:T(8,128)(2,1)}), bf16[256,768]{1,0:T(8,128)(2,1)}) %all-reduce.48.cloned.1.call-update) | async-done | bytes 393232 | tf_op jit(solution)/shard_map/psum | solution.py:9
  1909.3 5.5 convolution_subtract_fusion
  (98 shorter events, 25.8 us)
Async XLA Ops:
  17.0 4.9 copy-start
  17.0 54.4 %all-to-all-start = ((bf16[8,2,256,512]{3,2,1,0:T(8,128)(2,1)}), bf16[8,2,256,512]{3,2,1,0:T(8,128)(2,1)}, u32[]{:S(2)}, u32[]{:S(2)}) async-start(bf16[8,2,256,512]{3,2,1,0:T(8,128)(2,1)} %copy.33), calls=%async_computation | async-start | bytes 8388608 | tf_op jit(solution)/shard_map/all_to_all | solution.py:86
  166.1 464.3 %all-to-all-start.1 = ((bf16[16,2,1536,256]{3,1,2,0:T(2,128)(2,1)}), bf16[16,2,1536,256]{3,1,2,0:T(2,128)(2,1)}, u32[]{:S(2)}, u32[]{:S(2)}) async-start(bf16[16,2,1536,256]{3,1,2,0:T(2,128)(2,1)} %copy.39), calls=%async_computation.1 | async-start | bytes 50331648 | tf_op jit(solution)/shard_map/all_to_all | solution.py:104
  174.3 592.7 %all-reduce.18.cloned.1.call-start = ((), (), s32[]{:S(2)}) async-start(), calls=%async_computation.2 | async-start | bytes 1572864 | tf_op jit(solution)/shard_map/psum | solution.py:9
  677.0 152.4 %all-reduce.20.cloned.1.call-start = ((), (), s32[]{:S(2)}) async-start(), calls=%async_computation.3 | async-start | bytes 786432 | tf_op jit(solution)/shard_map/psum | solution.py:9
  677.9 243.6 %all-reduce.22.cloned.1.call-start = ((), (), s32[]{:S(2)}) async-start(), calls=%async_computation.4 | async-start | bytes 1572864 | tf_op jit(solution)/shard_map/psum | solution.py:9
  835.9 147.9 %all-reduce.24.cloned.1.call-start = ((), (), s32[]{:S(2)}) async-start(), calls=%async_computation.5 | async-start | bytes 786432 | tf_op jit(solution)/shard_map/psum | solution.py:9
  836.8 239.1 %all-reduce.26.cloned.1.call-start = ((), (), s32[]{:S(2)}) async-start(), calls=%async_computation.6 | async-start | bytes 1572864 | tf_op jit(solution)/shard_map/psum | solution.py:9
  990.3 147.9 %all-reduce.28.cloned.1.call-start = ((), (), s32[]{:S(2)}) async-start(), calls=%async_computation.7 | async-start | bytes 786432 | tf_op jit(solution)/shard_map/psum | solution.py:9
  991.1 239.0 %all-reduce.30.cloned.1.call-start = ((), (), s32[]{:S(2)}) async-start(), calls=%async_computation.8 | async-start | bytes 1572864 | tf_op jit(solution)/shard_map/psum | solution.py:9
  1144.6 148.0 %all-reduce.32.cloned.1.call-start = ((), (), s32[]{:S(2)}) async-start(), calls=%async_computation.9 | async-start | bytes 786432 | tf_op jit(solution)/shard_map/psum | solution.py:9
  1145.5 239.1 %all-reduce.34.cloned.1.call-start = ((), (), s32[]{:S(2)}) async-start(), calls=%async_computation.10 | async-start | bytes 1572864 | tf_op jit(solution)/shard_map/psum | solution.py:9
  1299.1 147.8 %all-reduce.36.cloned.1.call-start = ((), (), s32[]{:S(2)}) async-start(), calls=%async_computation.11 | async-start | bytes 786432 | tf_op jit(solution)/shard_map/psum | solution.py:9
  1299.9 239.0 %all-reduce.38.cloned.1.call-start = ((), (), s32[]{:S(2)}) async-start(), calls=%async_computation.12 | async-start | bytes 1572864 | tf_op jit(solution)/shard_map/psum | solution.py:9
  1453.4 147.9 %all-reduce.40.cloned.1.call-start = ((), (), s32[]{:S(2)}) async-start(), calls=%async_computation.13 | async-start | bytes 786432 | tf_op jit(solution)/shard_map/psum | solution.py:9
  1454.2 239.1 %all-reduce.42.cloned.1.call-start = ((), (), s32[]{:S(2)}) async-start(), calls=%async_computation.14 | async-start | bytes 1572864 | tf_op jit(solution)/shard_map/psum | solution.py:9
  1607.7 147.9 %all-reduce.44.cloned.1.call-start = ((), (), s32[]{:S(2)}) async-start(), calls=%async_computation.15 | async-start | bytes 786432 | tf_op jit(solution)/shard_map/psum | solution.py:9
  1608.6 239.1 %all-reduce.46.cloned.1.call-start = ((), (), s32[]{:S(2)}) async-start(), calls=%async_computation.16 | async-start | bytes 1572864 | tf_op jit(solution)/shard_map/psum | solution.py:9
  1762.1 147.3 %all-reduce.48.cloned.1.call-start = ((), (), s32[]{:S(2)}) async-start(), calls=%async_computation.17 | async-start | bytes 786432 | tf_op jit(solution)/shard_map/psum | solution.py:9
Sparse Core Ops, SparseCore 0:
  677.2 89.7 all-reduce.17
  770.0 59.4 all-reduce.19
  836.0 85.3 all-reduce.21
  924.3 59.4 all-reduce.23
  990.4 85.3 all-reduce.25
  1078.7 59.4 all-reduce.27
  1144.7 85.3 all-reduce.29
  1233.2 59.4 all-reduce.31
  1299.2 85.3 all-reduce.33
  1387.5 59.3 all-reduce.35
  1453.5 85.3 all-reduce.37
  1541.8 59.4 all-reduce.39
  1607.8 85.3 all-reduce.41
  1696.1 59.4 all-reduce.43
  1762.2 85.3 all-reduce.45
  1849.9 59.3 all-reduce.47
where the time goes:
time: 1930 us; the launch traced here: 1920 us
  waiting for transfers between devices  1660 us (86%)
  matrix products  138 us (7%)
  local copies, waits for them, and re-layouts  75.8 us (4%)
  other arithmetic  21.7 us (1%)
    psum x16, waiting for transfers between devices, broadcast(): return lax.psum(block, axis)  1160 us
    all_to_all x1, waiting for transfers between devices, per_device(): lax.all_to_all(col_send, 'col', split_axis=0, concat_axis=0, tiled=True)  454 us
    all_to_all x1, waiting for transfers between devices, per_device(): lax.all_to_all(row_send, 'row', split_axis=0, concat_axis=0, tiled=True)  45.8 us
    dot_general x8, matrix products, per_device(): jnp.dot(factor_block, row_panel, preferred_element_type=jnp.float32)  43.9 us
  transfers between devices with their start and end apart: 18, of which 18 were waited for; matrix products, arithmetic and copies ran while one was open for 2% of the time, Pallas kernels for 0%

commit v1 on v0

v1 whole, which is shorter than its diff:
```python
import functools

import jax
import jax.numpy as jnp
from jax import lax
from jax.experimental import pallas as pl
from jax.experimental.pallas import tpu as pltpu
from jax.sharding import PartitionSpec as P

MESH = pl.DeviceIdType.MESH
BF = jnp.bfloat16
F32 = jnp.float32
HBM = pl.BlockSpec(memory_space=pl.ANY)
VM = pl.BlockSpec(memory_space=pltpu.VMEM)
SM = pl.BlockSpec(memory_space=pltpu.SMEM)
DMA = pltpu.SemaphoreType.DMA


def sds(shape, dtype):
    return jax.ShapeDtypeStruct(shape, dtype)


def pack_kernel(maps, strips, out):
    r = lax.axis_index("row")
    k, s = r // 4, r % 4
    for x in range(4):
        start = jnp.int32(0)
        for i in range(8):
            start += (maps[k, s + 4 * i] < 12 * x).astype(jnp.int32)
        for slot in range(3):
            idx = jnp.minimum(start + slot, 7)
            for core in range(2):
                out[x, core, :, slot] = strips[idx, :, core]


def pack(maps, strips):
    return pl.pallas_call(
        pack_kernel,
        out_shape=sds((4, 2, 16, 3, 8, 512), BF),
        in_specs=[SM, VM],
        out_specs=VM,
        compiler_params=pltpu.CompilerParams(vmem_limit_bytes=24 << 20),
    )(maps, strips)


def front_kernel(fb, fl, lsem, ssem, rsem):
    r, c = lax.axis_index("row"), lax.axis_index("col")
    x, core = r // 2, r % 2
    me = c * 2 + core
    bar = pltpu.get_barrier_semaphore()

    def greet(i, n):
        d = lax.rem(me + i, 32)
        pl.semaphore_signal(
            bar, inc=1, device_id=(2 * x + lax.rem(d, 2), d // 2), device_id_type=MESH
        )
        return n

    lax.fori_loop(1, 32, greet, 0)
    pl.semaphore_wait(bar, 31)

    @pl.when(c < 3)
    def _():
        loc = pltpu.make_async_copy(
            fb.at[:, me], fl.at[jnp.minimum(c, 2), pl.ds(6 * core, 6)], lsem
        )
        loc.start()

        def send(i, n):
            d = lax.rem(me + i, 32)
            pltpu.make_async_remote_copy(
                fb.at[:, d],
                fl.at[jnp.minimum(c, 2), pl.ds(6 * core, 6)],
                ssem,
                rsem,
                device_id=(2 * x + lax.rem(d, 2), d // 2),
                device_id_type=MESH,
            ).start()
            return n

        lax.fori_loop(1, 32, send, 0)
        loc.wait()

        done = fb.at[:, pl.ds(0, 31)]
        pltpu.make_async_remote_copy(
            done, done, ssem, rsem, device_id=(r, c), device_id_type=MESH
        ).wait_send()
        part = fl.at[:, pl.ds(0, 10)]
        pltpu.make_async_remote_copy(
            part, part, ssem, rsem, device_id=(r, c), device_id_type=MESH
        ).wait_recv()

    @pl.when(c >= 3)
    def _():
        pltpu.make_async_remote_copy(
            fl, fl, ssem, rsem, device_id=(r, c), device_id_type=MESH
        ).wait_recv()


def front_scatter(fb):
    return pl.pallas_call(
        front_kernel,
        out_shape=sds((3, 12, 8, 768), BF),
        in_specs=[HBM],
        out_specs=HBM,
        scratch_shapes=[DMA, DMA, DMA],
        compiler_params=pltpu.CompilerParams(collective_id=1, has_side_effects=True),
    )(fb)


def sum_kernel(maps, recv, fl, cs, al, inv, rowt, cnt):
    x = lax.axis_index("row") // 2
    for k in range(2):

        def clear(t, n):
            inv[k, t] = -1
            return n

        lax.fori_loop(0, 48, clear, 0)

        def fill(a, n):
            inv[k, maps[k, a]] = a
            return n

        lax.fori_loop(0, 32, fill, 0)
        for s in range(4):
            start = jnp.int32(0)
            for i in range(8):
                start += (maps[k, s + 4 * i] < 12 * x).astype(jnp.int32)
            cnt[s] = start
        for pr in range(12):
            a = inv[k, 12 * x + pr]
            held = jnp.maximum(a, 0)
            s = held % 4
            rowt[k, pr] = jnp.where(a >= 0, (k * 4 + s) * 48 + held // 4 - cnt[s], -1)

    def column(pc, n):
        col = pl.ds(pl.multiple_of(pc * 256, 256), 256)
        b = [inv[k, pc] for k in range(2)]
        held = [jnp.maximum(v, 0) for v in b]
        for pr in range(12):
            total = None
            for k in range(2):
                row = rowt[k, pr]
                ok = (row >= 0) & (b[k] >= 0)
                idx = jnp.maximum(row, 0) + (held[k] % 16) * 3
                half = pl.multiple_of((held[k] // 16) * 256, 256)
                v = recv[idx, :, pl.ds(half, 256)].astype(F32)
                v = v * jnp.where(ok, 1.0, 0.0)
                total = v if total is None else total + v
            cs[pr, :, col] = total.astype(BF)
        return n

    lax.fori_loop(0, 48, column, 0)
    for c0 in range(3):
        w = min(768, 2048 - 768 * c0)
        for pr in range(12):
            part = cs[pr, :, 768 * c0 : 768 * c0 + w].astype(F32)
            al[pr, :, 768 * c0 : 768 * c0 + w] = (part + fl[c0, pr, :, :w].astype(F32)).astype(BF)


def child_sums(maps, recv, fl):
    return pl.pallas_call(
        sum_kernel,
        out_shape=(sds((12, 8, 12288), BF), sds((12, 8, 2048), BF)),
        in_specs=[SM, VM, VM],
        out_specs=(VM, VM),
        scratch_shapes=[
            pltpu.SMEM((2, 48), jnp.int32),
            pltpu.SMEM((2, 12), jnp.int32),
            pltpu.SMEM((4,), jnp.int32),
        ],
        compiler_params=pltpu.CompilerParams(vmem_limit_bytes=40 << 20),
    )(maps, recv, fl)


def exchange_kernel(cs, al, recv, blk, lsem, psem, prem, lsend, lrecv, csend, crecv):
    r, c = lax.axis_index("row"), lax.axis_index("col")
    x, core = r // 2, r % 2
    me = c * 2 + core
    bar = pltpu.get_barrier_semaphore()

    def greet(i, n):
        d = lax.rem(me + i, 32)
        pl.semaphore_signal(
            bar, inc=1, device_id=(2 * x + lax.rem(d, 2), d // 2), device_id_type=MESH
        )
        return n

    lax.fori_loop(1, 32, greet, 0)
    for dx in range(1, 4):
        for rho in range(2):
            pl.semaphore_signal(
                bar, inc=1, device_id=(2 * lax.rem(x + dx, 4) + rho, c), device_id_type=MESH
            )
    pl.semaphore_wait(bar, 31 + 6)

    def corner(rho, h, dev, to):
        return pltpu.make_async_remote_copy(
            al.at[pl.ds(4 * rho + 2 * h, 2)],
            blk.at[h, pl.ds(3, 2), pl.ds(pl.multiple_of(8 * core, 8), 8)],
            csend.at[to, h],
            crecv.at[core, h],
            device_id=dev,
            device_id_type=MESH,
        )

    def corner_from(frm, h):
        return pltpu.make_async_remote_copy(
            al.at[pl.ds(0, 2)],
            blk.at[h, pl.ds(3, 2), pl.ds(8 * frm, 8)],
            csend.at[0, h],
            crecv.at[frm, h],
            device_id=(r, c),
            device_id_type=MESH,
        )

    @pl.when(x == 0)
    def _():
        for dx in range(1, 4):
            for rho in range(2):
                for h in range(2):
                    corner(rho, h, (2 * dx + rho, c), 2 * dx + rho).start()
        for h in range(2):
            corner(1 - core, h, (1 - core, c), 0).start()
            pltpu.make_async_copy(
                al.at[pl.ds(4 * core + 2 * h, 2)],
                blk.at[h, pl.ds(3, 2), pl.ds(pl.multiple_of(8 * core, 8), 8)],
                lsem.at[2 + h],
            ).start()

    rows = pl.ds(pl.multiple_of(8 * core, 8), 8)
    swaps, keeps = [], []
    for h in range(2):
        cp = pltpu.make_async_remote_copy(
            al.at[pl.ds(6 * (1 - core) + 3 * h, 3)],
            blk.at[h, pl.ds(0, 3), rows],
            lsend.at[h],
            lrecv.at[h],
            device_id=(2 * x + 1 - core, c),
            device_id_type=MESH,
        )
        cp.start()
        swaps.append(cp)
        cp = pltpu.make_async_copy(
            al.at[pl.ds(6 * core + 3 * h, 3)], blk.at[h, pl.ds(0, 3), rows], lsem.at[h]
        )
        cp.start()
        keeps.append(cp)

    def mine(rho, d):
        return cs.at[pl.ds(6 * rho, 6), :, pl.ds(pl.multiple_of((d // 2) * 768, 768), 768)]

    own = pltpu.make_async_copy(mine(core, me), recv.at[:, me], lsem.at[4])
    own.start()

    def send(i, n):
        d = lax.rem(me + i, 32)
        rho = lax.rem(d, 2)
        pltpu.make_async_remote_copy(
            mine(rho, d),
            recv.at[:, me],
            psem,
            prem,
            device_id=(2 * x + rho, d // 2),
            device_id_type=MESH,
        ).start()
        return n

    lax.fori_loop(1, 32, send, 0)

    for cp in keeps:
        cp.wait()
    for cp in swaps:
        cp.wait()
    own.wait()

    @pl.when(x == 0)
    def _():
        for dx in range(1, 4):
            for rho in range(2):
                for h in range(2):
                    corner(rho, h, (2 * dx + rho, c), 2 * dx + rho).wait_send()
        for h in range(2):
            corner(1 - core, h, (1 - core, c), 0).wait_send()
            pltpu.make_async_copy(
                al.at[pl.ds(4 * core + 2 * h, 2)],
                blk.at[h, pl.ds(3, 2), pl.ds(pl.multiple_of(8 * core, 8), 8)],
                lsem.at[2 + h],
            ).wait()

    for frm in range(2):

        @pl.when((x > 0) | (core != frm))
        def _():
            for h in range(2):
                corner_from(frm, h).wait_recv()

    done = recv.at[:, pl.ds(0, 31)]
    pltpu.make_async_remote_copy(
        done, done, psem, prem, device_id=(r, c), device_id_type=MESH
    ).wait()


def exchange(cs, al):
    return pl.pallas_call(
        exchange_kernel,
        out_shape=(sds((6, 32, 8, 768), BF), sds((2, 5, 16, 2048), BF)),
        in_specs=[HBM, HBM],
        out_specs=(HBM, HBM),
        scratch_shapes=[
            DMA((5,)), DMA, DMA, DMA((2,)), DMA((2,)), DMA((8, 2)), DMA((2, 2)),
        ],
        compiler_params=pltpu.CompilerParams(collective_id=2, has_side_effects=True),
    )(cs, al)


def gather_kernel(blk, ar, g, gs, rg, lsem, s1, r1, s2, r2, ssib, rsib, sx, rx, sxs, rxs):
    r, c = lax.axis_index("row"), lax.axis_index("col")
    x, core = r // 2, r % 2
    y, z = c // 4, c % 4
    bar = pltpu.get_barrier_semaphore()
    sib = (2 * x + 1 - core, c)

    def cid(h, df, ds):
        dy, dz = (ds, df) if h == 0 else (df, ds)
        return lax.rem(y + dy + 4, 4) * 4 + lax.rem(z + dz + 4, 4)

    def xdev(dx):
        return (2 * lax.rem(x + dx + 4, 4) + core, c)

    partners = [sib, xdev(1), xdev(-1)]
    for d in (1, -1):
        partners += [(r, cid(0, d, 0)), (r, cid(0, 0, d))]
    for dev in partners:
        pl.semaphore_signal(bar, inc=1, device_id=dev, device_id_type=MESH)
    pl.semaphore_wait(bar, len(partners))

    sent = []

    def push(src, dst, ss, rs, dev):
        cp = pltpu.make_async_remote_copy(
            src, dst, ss, rs, device_id=dev, device_id_type=MESH
        )
        cp.start()
        sent.append(cp)

    def landed(dst, ss, rs):
        pltpu.make_async_remote_copy(
            dst, dst, ss, rs, device_id=sib, device_id_type=MESH
        ).wait_recv()

    locs = []
    for h in range(2):
        cp = pltpu.make_async_copy(blk.at[h], g.at[c, h], lsem.at[h])
        cp.start()
        locs.append(cp)

    cols = [pl.ds(0, 1024), pl.ds(1024, 1024)]
    order = (0, -1, 1, 2)

    def first(h):
        for n, d in enumerate((1, -1)):
            push(blk.at[h], g.at[c, h], s1.at[h, n], r1.at[h, n], (r, cid(h, d, 0)))

    def second(h, f):
        df = order[f]
        ident = cid(h, df, 0)
        src = blk.at[h] if df == 0 else g.at[ident, h]
        for n, d in enumerate((1, -1)):
            push(src, g.at[ident, h], s2.at[h, f, n], r2.at[h, f, n], (r, cid(h, 0, d)))

    def sibling(h, df, ds, n, own=False):
        ident = cid(h, df, ds)
        src = blk.at[h, pl.ds(3, 2)] if own else g.at[ident, h, pl.ds(3, 2)]
        push(src, gs.at[ident, h], ssib.at[h, n], rsib.at[h, n], sib)

    def relay_first(h, n):
        ident = cid(h, -1 if n == 0 else 1, 0)
        landed(g.at[ident, h], s1.at[h, n], r1.at[h, n])
        part = g.at[ident, h, :, :, cols[n]]
        push(part, part, s1.at[h, 2 + n], r1.at[h, 2 + n], (r, cid(h, 1 if n == 0 else -1, 0)))
        second(h, 1 + n)
        sibling(h, -1 if n == 0 else 1, 0, 1 + n)

    def finish_first(h):
        ident = cid(h, 2, 0)
        for n in range(2):
            landed(g.at[ident, h, :, :, cols[n]], s1.at[h, 2 + n], r1.at[h, 2 + n])
        second(h, 3)
        sibling(h, 2, 0, 3)

    def relay_second(h, f, n):
        ds = -1 if n == 0 else 1
        ident = cid(h, order[f], ds)
        landed(g.at[ident, h], s2.at[h, f, n], r2.at[h, f, n])
        part = g.at[ident, h, :, :, cols[n]]
        push(
            part, part, s2.at[h, f, 2 + n], r2.at[h, f, 2 + n],
            (r, cid(h, 0, 1 if n == 0 else -1)),
        )
        sibling(h, order[f], ds, 4 + 3 * f + n)

    def finish_second(h, f):
        ident = cid(h, order[f], 2)
        for n in range(2):
            landed(g.at[ident, h, :, :, cols[n]], s2.at[h, f, 2 + n], r2.at[h, f, 2 + n])
        sibling(h, order[f], 2, 4 + 3 * f + 2)

    for h in range(2):
        first(h)
    for h in range(2):
        second(h, 0)
        sibling(h, 0, 0, 0, own=True)

    def chunk(q):
        return rg.at[pl.ds(pl.multiple_of(512 * q, 512), 512)]

    def xcopy(src, dst, ss, rs, dev):
        return pltpu.make_async_remote_copy(
            src, dst, ss, rs, device_id=dev, device_id_type=MESH
        )

    def arow(q):
        return ar.at[pl.ds(512 * q, 512)]

    def zero_core0():
        out = [xcopy(arow(2), chunk(2), sxs.at[2], rxs.at[2], sib)]
        for u in range(2):
            for n, d in enumerate((1, -1)):
                out.append(xcopy(arow(u), chunk(u), sx.at[n, u], rx.at[u], xdev(d)))
            out.append(xcopy(arow(u), chunk(u), sxs.at[u], rxs.at[u], sib))
        return out

    def zero_core1():
        out = [
            xcopy(arow(0), chunk(3), sx.at[n, 1], rx.at[1], xdev(d))
            for n, d in enumerate((1, -1))
        ]
        out.append(xcopy(arow(0), chunk(3), sxs.at[1], rxs.at[1], sib))
        return out

    def zero_core1_late():
        return [
            xcopy(chunk(2), chunk(2), sx.at[n, 0], rx.at[0], xdev(d))
            for n, d in enumerate((1, -1))
        ]

    @pl.when((x == 0) & (core == 0))
    def _():
        pltpu.make_async_copy(ar, rg.at[pl.ds(0, 1536)], lsem.at[2]).start()
        for cp in zero_core0():
            cp.start()

    @pl.when((x == 0) & (core == 1))
    def _():
        pltpu.make_async_copy(arow(0), chunk(3), lsem.at[2]).start()
        for cp in zero_core1():
            cp.start()

    for n in range(2):
        for h in range(2):
            relay_first(h, n)

    @pl.when((x == 0) & (core == 1))
    def _():
        landed(chunk(2), sxs.at[2], rxs.at[2])
        for cp in zero_core1_late():
            cp.start()

    for n in range(2):
        for h in range(2):
            relay_second(h, 0, n)
    for h in range(2):
        finish_first(h)

    mine = 2 * core

    def onward(u):
        return xcopy(
            chunk(mine + u), chunk(mine + u), sx.at[0, u], rx.at[u], xdev(1 if u == 0 else -1)
        )

    def across(u):
        return xcopy(chunk(mine + u), chunk(mine + u), sxs.at[u], rxs.at[u], sib)

    for u, via in ((1, 3), (0, 1)):

        @pl.when((x == 1) | (x == 3))
        def _():
            landed(chunk(mine + u), sx.at[0, u], rx.at[u])
            across(u).start()

        @pl.when(x == via)
        def _():
            onward(u).start()

    for f in (1, 2):
        for n in range(2):
            for h in range(2):
                relay_second(h, f, n)
    for h in range(2):
        finish_second(h, 0)
    for n in range(2):
        for h in range(2):
            relay_second(h, 3, n)
    for f in (1, 2, 3):
        for h in range(2):
            finish_second(h, f)

    @pl.when(x == 2)
    def _():
        for u in range(2):
            landed(chunk(mine + u), sx.at[0, u], rx.at[u])
            across(u).start()

    @pl.when(x > 0)
    def _():
        for u in range(2):
            across(u).wait_send()
            landed(chunk(2 - mine + u), sxs.at[u], rxs.at[u])

    for u, via in ((0, 1), (1, 3)):

        @pl.when(x == via)
        def _():
            onward(u).wait_send()

    @pl.when((x == 0) & (core == 0))
    def _():
        pltpu.make_async_copy(ar, rg.at[pl.ds(0, 1536)], lsem.at[2]).wait()
        for cp in zero_core0():
            cp.wait_send()
        landed(chunk(3), sxs.at[1], rxs.at[1])

    @pl.when((x == 0) & (core == 1))
    def _():
        pltpu.make_async_copy(arow(0), chunk(3), lsem.at[2]).wait()
        for cp in zero_core1() + zero_core1_late():
            cp.wait_send()
        for u in range(2):
            landed(chunk(u), sxs.at[u], rxs.at[u])

    for cp in locs:
        cp.wait()
    for cp in sent:
        cp.wait_send()
    for h in range(2):
        for n, (df, ds) in enumerate(
            [(0, 0), (-1, 0), (1, 0), (2, 0)]
            + [(df, ds) for df in order for ds in (-1, 1, 2)]
        ):
            landed(gs.at[cid(h, df, ds), h], ssib.at[h, n], rsib.at[h, n])


def gather(blk, ar):
    return pl.pallas_call(
        gather_kernel,
        out_shape=(
            sds((16, 2, 5, 16, 2048), BF),
            sds((16, 2, 2, 16, 2048), BF),
            sds((2048, 768), BF),
        ),
        in_specs=[HBM, HBM],
        out_specs=(HBM, HBM, HBM),
        scratch_shapes=[
            DMA((3,)),
            DMA((2, 4)), DMA((2, 4)),
            DMA((2, 4, 4)), DMA((2, 4, 4)),
            DMA((2, 16)), DMA((2, 16)),
            DMA((2, 2)), DMA((2,)),
            DMA((3,)), DMA((3,)),
        ],
        compiler_params=pltpu.CompilerParams(collective_id=3, has_side_effects=True),
    )(blk, ar)


def eliminate_kernel(g, gs, rg, cs, front, pinv, out, factor, xs, rr, sem):
    r, c = lax.axis_index("row"), lax.axis_index("col")
    core = r % 2
    loads = []
    for pr in range(8):
        h, u = (pr % 4) // 2, pr % 2
        for src, side in ((g, pr // 4), (gs, 1 - pr // 4)):
            unit = 3 + u if src is g else u

            @pl.when(core == side)
            def _():
                pltpu.make_async_copy(src.at[:, h, unit], xs.at[pr], sem.at[pr]).start()

    for t in range(6):
        pltpu.make_async_copy(g.at[:, t // 3, t % 3], xs.at[8 + t], sem.at[8 + t]).start()
    pltpu.make_async_copy(rg, rr, sem.at[14]).start()
    for t in range(14):
        pltpu.make_async_copy(g.at[:, 0, 0], xs.at[t], sem.at[t]).wait()
    pltpu.make_async_copy(rg, rr, sem.at[14]).wait()

    def rows(t, lo, hi):
        return xs[t, :, :, lo:hi].reshape(256, hi - lo)

    for j in range(8):
        lo, hi = 256 * j, 256 * (j + 1)

        def panel(t, n):
            acc = rows(t, lo, hi).astype(F32)
            if j:
                upper = xs[0:j, :, :, lo:hi].reshape(lo, 256)
                acc = acc - jnp.dot(rows(t, 0, lo), upper, preferred_element_type=F32)
            block = jnp.dot(acc.astype(BF), pinv[j], preferred_element_type=F32)
            xs[t, :, :, lo:hi] = block.astype(BF).reshape(16, 16, 256)
            return n

        lax.fori_loop(j + 1, 14, panel, 0)
        if j:
            left = rows(j, 0, lo)
            for m in range(j + 1, 8):
                cols = slice(256 * m, 256 * (m + 1))
                acc = rows(j, 256 * m, 256 * (m + 1)).astype(F32)
                upper = xs[0:j, :, :, cols].reshape(lo, 256)
                acc = acc - jnp.dot(left, upper, preferred_element_type=F32)
                xs[j, :, :, cols] = acc.astype(BF).reshape(16, 16, 256)
            acc = rr[lo:hi].astype(F32) - jnp.dot(left, rr[0:lo], preferred_element_type=F32)
            rr[lo:hi] = acc.astype(BF)

    mycols = pl.ds(pl.multiple_of(c * 128, 128), 128)

    def update(t, n):
        at = pl.ds(pl.multiple_of(t * 256, 256), 256)
        prod = jnp.dot(rows(8 + t, 0, 2048), rr[...], preferred_element_type=F32)
        out[at, :] = front[at, :] + cs[at, :].astype(F32) - prod
        factor[at, :] = xs[8 + t, :, :, mycols].reshape(256, 128)
        return n

    lax.fori_loop(0, 6, update, 0)


def eliminate(g, gs, rg, cs, front, pinv):
    return pl.pallas_call(
        eliminate_kernel,
        out_shape=(sds((1536, 768), F32), sds((1536, 128), BF)),
        in_specs=[HBM, HBM, HBM, VM, VM, VM],
        out_specs=(VM, VM),
        scratch_shapes=[
            pltpu.VMEM((14, 16, 16, 2048), BF),
            pltpu.VMEM((2048, 768), BF),
            DMA((15,)),
        ],
        compiler_params=pltpu.CompilerParams(vmem_limit_bytes=60 << 20),
    )(g, gs, rg, cs, front, pinv)


def per_device(child_update, front, pivot_inverses, child_maps):
    strips = child_update[0].reshape(8, 16, 2, 8, 512)
    send = pack(child_maps, strips)
    fb = front.astype(BF).reshape(6, 32, 8, 768)
    recv = lax.all_to_all(
        send.reshape(128, 3, 8, 512), ("row", "col"), split_axis=0, concat_axis=0, tiled=True
    )
    fl = front_scatter(fb)
    cs, al = child_sums(child_maps, recv.reshape(384, 8, 512), fl)
    own, blk = exchange(cs, al)
    own = own.reshape(1536, 768)
    ar = (front + own.astype(F32)).astype(BF)
    g, gs, rg = gather(blk, ar)
    return eliminate(g, gs, rg, own, front, pivot_inverses)


def solution(mesh):
    placed = (P("row", None, None, None, "col"), P("row", "col"), P(), P())
    return jax.shard_map(
        per_device,
        mesh=mesh,
        in_specs=placed,
        out_specs=(P("row", "col"), P("row", "col")),
        check_vma=False,
    )
```

time: 1930 us -> 292 us (0.15)
  waiting for transfers between devices: 1660 us -> 0.01 us
  Pallas kernels: 0 us -> 262 us
  matrix products: 138 us -> 0 us
  local copies, waits for them, and re-layouts: 75.8 us -> 7.97 us
    psum x16 -> x0, waiting for transfers between devices: 1160 us -> none  [broadcast(): return lax.psum(block, axis)]
    all_to_all x2 -> x1, waiting for transfers between devices: 500 us -> 0.01 us  [per_device(): lax.all_to_all(send.reshape(128, 3, 8, 512), ('row', 'col'), split_axis=0...]
    pallas_call x0 -> x6, Pallas kernels: none -> 262 us  [the longest x1 96.6 us: gather(): pl.pallas_call(gather_kernel, out_shape=(sds((16, 2, 5, 16, 2048), BF), s...]
    dot_general x21 -> x0, matrix products: 138 us -> none  [the longest x8 43.9 us: per_device(): jnp.dot(factor_block, row_panel, preferred_element_type=jnp.float32)]
    convert_element_type x3 -> x0, local copies, waits for them, and re-layouts: 39.4 us -> none  [the longest x1 35.9 us: per_device(): col_send = jnp.einsum('kdh,kphq->dkpq', outgoing, per_child, preferred_el...]
  transfers between devices with their start and end apart: 18 -> 1, of which waited for: 18 -> 0; matrix products, arithmetic and copies ran while one was open for 2% -> 1% of each run, Pallas kernels for 0% -> 19%
where the time goes in v1:
time: 292 us; the launch traced here: 291 us
  Pallas kernels  262 us (90%)
  starting transfers between devices  11.1 us (4%)
  other arithmetic  9 us (3%)
  local copies, waits for them, and re-layouts  7.97 us (3%)
    pallas_call x1, Pallas kernels, gather(): pl.pallas_call(gather_kernel, out_shape=(sds((16, 2, 5, 16, 2048), BF), s...  96.6 us
    pallas_call x1, Pallas kernels, front_scatter(): pl.pallas_call(front_kernel, out_shape=sds((3, 12, 8, 768), BF), in_specs...  54.9 us
    pallas_call x1, Pallas kernels, eliminate(): pl.pallas_call(eliminate_kernel, out_shape=(sds((1536, 768), F32), sds((1...  54.2 us
    pallas_call x1, Pallas kernels, exchange(): pl.pallas_call(exchange_kernel, out_shape=(sds((6, 32, 8, 768), BF), sds(...  48.7 us
    all_to_all x1, starting transfers between devices, per_device(): lax.all_to_all(send.reshape(128, 3, 8, 512), ('row', 'col'), split_axis=0...  11.1 us
    pallas_call x1, Pallas kernels, child_sums(): pl.pallas_call(sum_kernel, out_shape=(sds((12, 8, 12288), BF), sds((12, 8...  6.71 us
  transfers between devices with their start and end apart: 1, of which 0 were waited for; matrix products, arithmetic and copies ran while one was open for 1% of the time, Pallas kernels for 19%

profile of v1, /device:TPU:0, one launch (start us, length us, event | category | flops | bytes accessed | tf_op | source)
XLA Modules:
  0.0 290.9 jit_solution(15967797265414492797)
XLA Ops:
  0.6 0.0 copy-start.4
  0.6 3.2 %reshape_squeeze.3.strips = bf16[8,16,2,8,512]{4,3,2,1,0:T(8,128)(2,1)S(1)} reshape(bf16[1,8,256,2,256]{4,3,2,1,0:T(2,128)(2,1)} %param.4) | data formatting | bytes 4194304 | tf_op jit(solution)/shard_map/reshape;squeeze | solution.py:653
  3.8 0.0 copy-done.4
  3.8 0.8 shard_map.59
  4.6 0.0 copy-start
  4.6 1.7 copy-done
  6.3 11.1 %all-to-all-start = ((bf16[128,3,8,512]{3,2,1,0:T(8,128)(2,1)}), bf16[128,3,8,512]{3,2,1,0:T(8,128)(2,1)S(1)}, u32[]{:S(2)}, u32[]{:S(2)}) async-start(bf16[128,3,8,512]{3,2,1,0:T(8,128)(2,1)} %bitcast.6), calls=%async_computation | async-start | bytes 6291456 | tf_op jit(solution)/shard_map/all_to_all | solution.py:656
  17.4 4.0 %convert_element_type.9 = bf16[1536,768]{1,0:T(8,128)(2,1)} convert(f32[1536,768]{1,0:T(8,128)} %front.1) | non-fusion elementwise | flops 1179648 | bytes 7077888 | tf_op jit(solution)/shard_map/convert_element_type | solution.py:655
  21.4 54.9 %shard_map.60.fl = bf16[3,12,8,768]{3,2,1,0:T(8,128)(2,1)} custom-call(bf16[6,32,8,768]{3,2,1,0:T(8,128)(2,1)} %bitcast.8), custom_call_target="tpu_custom_call" | custom-call | tf_op jit(solution)/shard_map/pallas_call | solution.py:101
  76.4 0.0 all-to-all-done
  76.4 0.0 copy-start.2
  76.4 1.0 copy-done.2
  77.4 6.7 %shard_map.61 = (bf16[12,8,12288]{2,1,0:T(8,128)(2,1)S(1)}, bf16[12,8,2048]{2,1,0:T(8,128)(2,1)S(1)}) custom-call(s32[2,32]{1,0:T(2,128)S(1)} %copy-done.4, bf16[384,8,512]{2,1,0:T(8,128)(2,1)S(1)} %bitcast.5, bf16[3,12,8,768]{3,2,1,0:T(8,128)(2,1)S(1)} %copy-done.2), custom_call_target="tpu_custom_call" | custom-call | tf_op jit(solution)/shard_map/pallas_call | solution.py:163
  84.1 0.0 copy-start.1
  84.1 1.4 copy-done.1
  85.5 0.0 copy-start.3
  85.5 0.7 copy-done.3
  86.3 48.7 %shard_map.62 = (bf16[6,32,8,768]{3,2,1,0:T(8,128)(2,1)}, bf16[2,5,16,2048]{3,2,1,0:T(8,128)(2,1)}) custom-call(bf16[12,8,12288]{2,1,0:T(8,128)(2,1)} %copy-done.1, bf16[12,8,2048]{2,1,0:T(8,128)(2,1)} %copy-done.3), custom_call_target="tpu_custom_call" | custom-call | tf_op jit(solution)/shard_map/pallas_call | solution.py:306
  135.0 5.0 %add_convert_fusion.ar = bf16[1536,768]{1,0:T(8,128)(2,1)} fusion(f32[1536,768]{1,0:T(8,128)} %front.1, bf16[6,32,8,768]{3,2,1,0:T(8,128)(2,1)} %get-tuple-element.12), kind=kLoop, calls=%fused_computation | loop fusion | flops 3538944 | bytes 9437184 | tf_op jit(solution)/shard_map/convert_element_type | solution.py:663
  140.0 96.6 %shard_map.63 = (bf16[16,2,5,16,2048]{4,3,2,1,0:T(8,128)(2,1)}, bf16[16,2,2,16,2048]{4,3,2,1,0:T(8,128)(2,1)}, bf16[2048,768]{1,0:T(8,128)(2,1)}) custom-call(bf16[2,5,16,2048]{3,2,1,0:T(8,128)(2,1)} %get-tuple-element.11.blk, bf16[1536,768]{1,0:T(8,128)(2,1)} %add_convert_fusion.ar), custom_call_target="tpu_custom_call" | custom-call | tf_op jit(solution)/shard_map/pallas_call | solution.py:557
  236.6 54.2 %shard_map.64 = (f32[1536,768]{1,0:T(8,128)}, bf16[1536,128]{1,0:T(8,128)(2,1)}) custom-call(bf16[16,2,5,16,2048]{4,3,2,1,0:T(8,128)(2,1)} %get-tuple-element.13.g, bf16[16,2,2,16,2048]{4,3,2,1,0:T(8,128)(2,1)} %get-tuple-element.14.gs, bf16[2048,768]{1,0:T(8,128)(2,1)} %get-tuple-element.15.rg, bf16[1536,768]{1,0:T(8,128)(2,1)} %bitcast.7, ...), custom_call_target="tpu_custom_call" | custom-call | tf_op jit(solution)/shard_map/pallas_call | solution.py:638
Async XLA Ops:
  0.6 3.2 %copy-start.4 = (s32[2,32]{1,0:T(2,128)S(1)}, s32[2,32]{1,0:T(2,128)}, u32[]{:S(2)}) copy-start(s32[2,32]{1,0:T(2,128)} %maps.3) | copy-start | bytes 772
  4.6 1.7 copy-start
  6.3 70.1 %all-to-all-start = ((bf16[128,3,8,512]{3,2,1,0:T(8,128)(2,1)}), bf16[128,3,8,512]{3,2,1,0:T(8,128)(2,1)S(1)}, u32[]{:S(2)}, u32[]{:S(2)}) async-start(bf16[128,3,8,512]{3,2,1,0:T(8,128)(2,1)} %bitcast.6), calls=%async_computation | async-start | bytes 6291456 | tf_op jit(solution)/shard_map/all_to_all | solution.py:656
  76.4 1.0 copy-start.2
  84.1 1.4 copy-start.1
  85.5 0.7 copy-start.3
